TPU v7x, 512 devices: a whole 4x8x8 slice. The times are simulated.
512 devices in a mesh: crop: 16 (over z, core), dap: 32 (over y, x).
Axes of the slice: x: 4, y: 8, z: 8, core: 2. Of those that a mesh axis runs over, the one named last changes fastest.
Arguments:
- homolog_features: bfloat16 [2048, 128, 256], P(('crop', 'dap')), parts along dimension 0, may hold values from -6 to 6
- twofold_features: bfloat16 [2048, 128, 128], P(('crop', 'dap')), parts along dimension 0, may hold values from -6 to 6
- twofold_offset_map: bfloat16 [128, 8], replicated, may hold values from -0.5 to 0.5
- horizontal_attend_entry_maps: bfloat16 [256, 1024], replicated, may hold values from -2 to 2
- horizontal_attend_exit_map: bfloat16 [256, 256], replicated, may hold values from -0.375 to 0.375
- vertical_attend_entry_maps: bfloat16 [256, 1024], replicated, may hold values from -2 to 2
- vertical_attend_exit_map: bfloat16 [256, 256], replicated, may hold values from -0.375 to 0.375
- tensor_product_factors: bfloat16 [256, 64], replicated, may hold values from -0.375 to 0.375
- tensor_product_exit_map: bfloat16 [1024, 128], replicated, may hold values from -1 to 1
Outputs:
- alignment_output: bfloat16 [2048, 128, 256], P('crop', 'dap'), parts along dimension 0
- pair_output: bfloat16 [2048, 128, 128], P(('crop', 'dap')), parts along dimension 0
There are 16 independent parts, one for each index of `crop`. A program takes and returns all parts, laid end to end along the dimension named above; an argument that names none is the same for every part. Nothing has to cross between parts.
All inputs are finite; a program needn't handle non-finite values.
Results may differ from a plain program's by a relative error of at most 0.0085.
Values may be sent and summed in bfloat16 or wider, within the bound.
A program may use at most 64 MiB of HBM per device.

v0:
```python
import math

import jax
import jax.numpy as jnp
from jax import lax
from jax.sharding import PartitionSpec as P

EPSILON = 1e-05


def joined_along(tiles, dim):
    tiles = jnp.moveaxis(tiles, 0, dim)
    dims = tiles.shape
    return tiles.reshape(*dims[:dim], dims[dim] * dims[dim + 1], *dims[dim + 2 :])


def copy_for_each(array, axis):
    length = lax.axis_size(axis)
    return lax.all_to_all(
        jnp.broadcast_to(array[None], (length, *array.shape)), axis, 0, 0, tiled=True
    )


def gathered_copies(array, axis, dim):
    return joined_along(copy_for_each(array, axis), dim)


def standardize_features(values):
    values = values.astype(jnp.float32)
    center = values - jnp.mean(values, axis=-1, keepdims=True)
    spread = jnp.mean(center * center, axis=-1, keepdims=True)
    return center * lax.rsqrt(spread + EPSILON)


def split_heads(packed, head_count):
    pieces = jnp.split(packed, 4, axis=-1)
    return [
        piece.reshape(piece.shape[:-1] + (head_count, piece.shape[-1] // head_count))
        for piece in pieces
    ]


def attend(queries, key_rows, value_rows, gate_rows, pair_bias):
    head_size = queries.shape[-1]
    scores = jnp.einsum(
        "bihd,bjhd->bhij", queries, key_rows, preferred_element_type=jnp.float32
    ) / math.sqrt(head_size)
    scores = scores + pair_bias
    highest = jnp.max(scores, axis=-1, keepdims=True)
    expo = jnp.exp(scores - highest)
    weights = (expo / jnp.sum(expo, axis=-1, keepdims=True)).astype(jnp.bfloat16)
    attended = jnp.einsum(
        "bhij,bjhd->bihd", weights, value_rows, preferred_element_type=jnp.float32
    )
    gated = (jax.nn.sigmoid(gate_rows.astype(jnp.float32)) * attended).astype(jnp.bfloat16)
    return gated.reshape(gated.shape[:2] + (gated.shape[2] * gated.shape[3],))


def mapped_horizontal_piece(homolog_features, horizontal_attend_entry_maps):
    horizontal_standardized = standardize_features(homolog_features).astype(jnp.bfloat16)
    return jnp.einsum(
        "src,cf->srf",
        horizontal_standardized,
        horizontal_attend_entry_maps,
        preferred_element_type=jnp.float32,
    ).astype(jnp.bfloat16)


def collect_bias(twofold_features, twofold_offset_map):
    pair_norm = standardize_features(twofold_features).astype(jnp.bfloat16)
    local_bias = jnp.einsum(
        "ijz,zh->hij", pair_norm, twofold_offset_map, preferred_element_type=jnp.float32
    ).astype(jnp.bfloat16)
    return gathered_copies(local_bias, "dap", 1)


def column_delta(received_blocks, vertical_attend_entry_maps, vertical_attend_exit_map, head_count):
    column_alignment = received_blocks[:, 0]
    column_layer_norm = standardize_features(column_alignment).astype(jnp.bfloat16)
    col_proj = jnp.einsum(
        "skc,cf->ksf",
        column_layer_norm,
        vertical_attend_entry_maps,
        preferred_element_type=jnp.float32,
    ).astype(jnp.bfloat16)
    queries, key_rows, value_rows, gate_rows = split_heads(col_proj, head_count)
    column_gated_output = attend(queries, key_rows, value_rows, gate_rows, 0.0)
    residual_delta = jnp.einsum(
        "ksf,fc->skc",
        column_gated_output,
        vertical_attend_exit_map,
        preferred_element_type=jnp.float32,
    )
    return (column_alignment.astype(jnp.float32) + residual_delta).astype(jnp.bfloat16)


def per_device(
    homolog_features,
    twofold_features,
    twofold_offset_map,
    horizontal_attend_entry_maps,
    horizontal_attend_exit_map,
    vertical_attend_entry_maps,
    vertical_attend_exit_map,
    tensor_product_factors,
    tensor_product_exit_map,
):
    head_count = twofold_offset_map.shape[1]
    horizontal_mapped_features = mapped_horizontal_piece(
        homolog_features, horizontal_attend_entry_maps
    )
    gathered = collect_bias(twofold_features, twofold_offset_map)
    bias_wide = gathered.astype(jnp.float32)[None]
    heads_row = split_heads(horizontal_mapped_features, head_count)

    def one_sequence(items):
        return attend(items[0][None], items[1][None], items[2][None], items[3][None], bias_wide)[0]

    horizontal_sigmoid_scaled = lax.map(one_sequence, tuple(heads_row))
    homolog_line = (
        homolog_features.astype(jnp.float32)
        + jnp.einsum(
            "asd,dy->asy",
            horizontal_sigmoid_scaled,
            horizontal_attend_exit_map,
            preferred_element_type=jnp.float32,
        )
    ).astype(jnp.bfloat16)
    parallel_width = lax.axis_size("dap")
    sequence_local, residue_total, channel_count = homolog_line.shape
    alignment_blocks = homolog_line.reshape(
        sequence_local, parallel_width, residue_total // parallel_width, channel_count
    )
    alignment_output = column_delta(
        lax.all_to_all(alignment_blocks, "dap", split_axis=1, concat_axis=0, tiled=True),
        vertical_attend_entry_maps,
        vertical_attend_exit_map,
        head_count,
    )
    outer_width = tensor_product_factors.shape[1] // 2
    homolog_tally = alignment_output.shape[0]
    residue_local = alignment_output.shape[1]
    outer_layer_norm = standardize_features(alignment_output).astype(jnp.bfloat16)
    left_rows = jnp.einsum(
        "src,cf->rsf",
        outer_layer_norm,
        tensor_product_factors[:, :outer_width],
        preferred_element_type=jnp.float32,
    ).astype(jnp.bfloat16)
    right_rows = jnp.einsum(
        "src,cf->rsf",
        outer_layer_norm,
        tensor_product_factors[:, outer_width:],
        preferred_element_type=jnp.float32,
    ).astype(jnp.bfloat16)
    right_flat = right_rows.reshape(residue_local, homolog_tally * outer_width)
    segment = gathered_copies(right_flat, "dap", 0)
    count_rows = segment.shape[0]
    right_three = segment.reshape(count_rows, homolog_tally, outer_width)
    product = (
        jnp.einsum("isc,jse->ijce", left_rows, right_three, preferred_element_type=jnp.float32)
        / homolog_tally
    )
    flat = product.astype(jnp.bfloat16).reshape(
        residue_local * count_rows, outer_width * outer_width
    )
    residual_delta = jnp.dot(flat, tensor_product_exit_map, preferred_element_type=jnp.float32)
    residual_delta = residual_delta.reshape(residue_local, count_rows, residual_delta.shape[-1])
    base_rows = twofold_features.astype(jnp.float32)
    pair_output = (base_rows + residual_delta).astype(jnp.bfloat16)
    return (alignment_output, pair_output)


def solution(mesh):
    in_specs = (
        P(("crop", "dap"), None, None),
        P(("crop", "dap"), None, None),
        P(),
        P(),
        P(),
        P(),
        P(),
        P(),
        P(),
    )
    out_specs = (P("crop", "dap", None), P(("crop", "dap"), None, None))
    return jax.shard_map(
        per_device, mesh=mesh, in_specs=in_specs, out_specs=out_specs, check_vma=False
    )
```

profile of v0, /device:TPU:448, one launch (start us, length us, event | category | flops | bytes accessed | tf_op | source)
XLA Modules:
  0.0 99.4 jit_solution(1011496540577789184)
XLA Ops:
  0.6 1.1 %convert_reduce_fusion.2 = f32[4,128]{1,0:T(4,128)S(1)} fusion(bf16[4,128,128]{2,1,0:T(8,128)(2,1)} %param.12), kind=kLoop, calls=%fused_computation.68 | loop fusion | flops 130560 | bytes 133120 | tf_op jit(solution)/shard_map/reduce_sum | solution.py:30
  1.7 1.1 %fusion.48 = f32[4,128]{1,0:T(4,128)S(1)} fusion(bf16[4,128,128]{2,1,0:T(8,128)(2,1)} %param.12, f32[4,128]{1,0:T(4,128)S(1)} %broadcast_multiply_fusion.2), kind=kLoop, calls=%fused_computation.71 | loop fusion | flops 261632 | bytes 135168 | tf_op jit(solution)/shard_map/reduce_sum | solution.py:31
  2.9 1.2 %fusion.32 = bf16[8,4,128]{2,0,1:T(8,128)(2,1)S(1)} fusion(bf16[4,128,128]{2,1,0:T(8,128)(2,1)} %param.12, f32[4,128]{1,0:T(4,128)S(1)} %add_rsqrt_fusion.2, f32[4,128]{1,0:T(4,128)S(1)} %broadcast_multiply_fusion.2, bf16[128,8]{0,1:T(8,128)(2,1)} %param.13), kind=kOutput, calls=%fused_computation.45 | convolution fusion | flops 1314816 | bytes 145408 | tf_op jit(solution)/shard_map/ijz,zh->hij/dot_general | solution.py:71
  4.1 0.7 broadcast_in_dim.12
  4.9 9.9 %all-to-all-start = ((bf16[32,8,4,128]{3,1,2,0:T(8,128)(2,1)}), bf16[32,8,4,128]{3,1,2,0:T(8,128)(2,1)S(1)}, u32[]{:S(2)}, u32[]{:S(2)}) async-start(bf16[32,8,4,128]{3,1,2,0:T(8,128)(2,1)} %broadcast_in_dim.12), calls=%async_computation | async-start | bytes 524288 | tf_op jit(solution)/shard_map/all_to_all | solution.py:19
  14.8 1.1 %convert_reduce_fusion = f32[4,128]{1,0:T(4,128)S(1)} fusion(bf16[4,128,256]{2,1,0:T(8,128)(2,1)} %param.11), kind=kLoop, calls=%fused_computation.48 | loop fusion | flops 261632 | bytes 264192 | tf_op jit(solution)/shard_map/reduce_sum | solution.py:30
  15.9 1.2 %fusion.38 = f32[4,128]{1,0:T(4,128)S(1)} fusion(bf16[4,128,256]{2,1,0:T(8,128)(2,1)} %param.11, f32[4,128]{1,0:T(4,128)S(1)} %broadcast_multiply_fusion.3), kind=kLoop, calls=%fused_computation.55 | loop fusion | flops 523776 | bytes 266240 | tf_op jit(solution)/shard_map/reduce_sum | solution.py:31
  17.2 1.4 %convolution_convert_fusion.1 = bf16[4,128,1024]{2,1,0:T(8,128)(2,1)S(1)} fusion(bf16[256,1024]{1,0:T(8,128)(2,1)S(1)} %copy-done, bf16[4,128,256]{2,1,0:T(8,128)(2,1)} %param.11, f32[4,128]{1,0:T(4,128)S(1)} %add_rsqrt_fusion.3, f32[4,128]{1,0:T(4,128)S(1)} %broadcast_multiply_fusion.3), kind=kOutput, calls=%fused_computation.27 | convolution fusion | flops 269484032 | bytes 1839104 | tf_op jit(solution)/shard_map/src,cf->srf/dot_general | solution.py:61
  18.6 0.1 fusion.80
  18.7 0.2 copy.76
  18.9 0.2 copy.77
  19.1 0.2 copy.74
  19.3 0.2 copy.75
  19.4 8.2 %all-to-all-done = bf16[32,8,4,128]{3,1,2,0:T(8,128)(2,1)S(1)} async-done(((bf16[32,8,4,128]{3,1,2,0:T(8,128)(2,1)}), bf16[32,8,4,128]{3,1,2,0:T(8,128)(2,1)S(1)}, u32[]{:S(2)}, u32[]{:S(2)}) %all-to-all-start) | async-done | bytes 262176 | tf_op jit(solution)/shard_map/all_to_all | solution.py:19
  27.7 0.2 copy.78
  28.0 3.8 %while.10 = (s32[]{:T(128)}, bf16[4,128,256]{1,2,0:T(8,128)(2,1)S(1)}, bf16[4,128,8,32]{1,3,2,0:T(8,128)(2,1)S(1)}, bf16[4,128,8,32]{1,3,2,0:T(8,128)(2,1)S(1)},...) while((s32[]{:T(128)}, ...), condition=%wide.region_7.8_spmd, body=%wide.region_4.7_spmd.sunk | while | flops 26543360 | bytes 3222617 | solution.py:119
  28.0 0.3 fusion.106
  28.3 0.4 fusion.105
  28.6 0.2 fusion.107
  28.9 0.3 fusion.106
  29.2 0.4 fusion.105
  29.6 0.2 fusion.107
  29.9 0.3 fusion.106
  30.2 0.4 fusion.105
  30.5 0.2 fusion.107
  30.8 0.3 fusion.106
  31.1 0.4 fusion.105
  31.5 0.2 fusion.107
  31.8 0.3 fusion.27
  32.1 0.1 copy.80
  32.2 16.2 %all_to_all.19 = bf16[4,32,4,256]{3,2,0,1:T(4,128)(2,1)S(1)} all-to-all(bf16[4,32,4,256]{3,2,0,1:T(4,128)(2,1)S(1)} %copy.80), channel_id=1, replica_groups=mesh['crop'=16,'dap'=32] {'dap'}, dimensions={1} | all-to-all | bytes 524288 | tf_op jit(solution)/shard_map/all_to_all | solution.py:135
  48.4 0.3 bitcast_reduce_fusion
  48.7 0.1 copy.83
  48.8 0.1 copy.85
  48.9 0.1 copy.84
  49.0 0.5 fusion.44
  49.5 0.1 copy.87
  49.6 0.1 copy.88
  49.7 0.1 rsqrt.38
  49.9 0.1 div.69
  50.0 0.1 bitcast_convert_fusion
  50.1 0.5 fusion.22
  50.6 0.1 fusion.79
  50.7 0.1 add_divide_fusion
  50.9 0.2 copy.91
  51.0 0.2 copy.92
  51.2 0.2 copy.90
  51.4 0.2 copy.89
  51.6 2.2 %fusion.81 = (f32[4,8,128]{2,1,0:T(8,128)S(1)}, f32[4,8,128,128]{2,3,1,0:T(8,128)}) fusion(bf16[4,128,8,32]{1,3,2,0:T(8,128)(2,1)S(1)} %bitcast.156, bf16[4,128,8,32]{1,3,2,0:T(8,128)(2,1)S(1)} %bitcast.157), kind=kOutput, calls=%fused_computation.101 | convolution fusion | flops 35127424 | bytes 2637824 | tf_op jit(solution)/shard_map/sub | solution.py:50
  53.8 2.0 %fusion.26 = bf16[4,128,8,32]{1,3,2,0:T(8,128)(2,1)S(1)} fusion(f32[4,128,8,32]{1,3,2,0:T(8,128)S(1)} %bitcast.153, bf16[4,128,8,32]{1,3,2,0:T(8,128)(2,1)S(1)} %bitcast.158, f32[4,8,128,128]{2,3,1,0:T(8,128)} %get-tuple-element.98, f32[4,8,128]{2,1,0:T(8,128)S(1)} %get-tuple-element.97), kind=kOutput, calls=%fused_computation.35 | convolution fusion | flops 34865152 | bytes 3162112 | tf_op jit(solution)/shard_map/bhij,bjhd->bihd/dot_general | solution.py:52
  55.9 0.4 convert_reduce_fusion.1
  56.3 0.2 fusion.40
  56.5 0.3 fusion.30
  56.9 0.1 copy.95
  57.0 0.2 broadcast_in_dim.13
  57.2 1.5 %broadcast_in_dim.14 = bf16[32,4,4096]{2,1,0:T(4,128)(2,1)} broadcast(bf16[4,4096]{1,0:T(4,128)(2,1)S(1)} %broadcast_in_dim.13), dimensions={1,2} | broadcast | bytes 1081344 | tf_op jit(solution)/shard_map/broadcast_in_dim | solution.py:20
  58.7 3.9 %all-to-all-start.2 = ((bf16[32,4,4096]{2,1,0:T(4,128)(2,1)}), bf16[32,4,4096]{2,1,0:T(4,128)(2,1)S(1)}, u32[]{:S(2)}, u32[]{:S(2)}) async-start(bf16[32,4,4096]{2,1,0:T(4,128)(2,1)} %broadcast_in_dim.14), calls=%async_computation.2 | async-start | bytes 2097152 | tf_op jit(solution)/shard_map/all_to_all | solution.py:19
  62.6 0.9 copy.99
  63.5 25.5 %all-to-all-done.2 = bf16[32,4,4096]{2,1,0:T(4,128)(2,1)S(1)} async-done(((bf16[32,4,4096]{2,1,0:T(4,128)(2,1)}), bf16[32,4,4096]{2,1,0:T(4,128)(2,1)S(1)}, u32[]{:S(2)}, u32[]{:S(2)}) %all-to-all-start.2) | async-done | bytes 1048608 | tf_op jit(solution)/shard_map/all_to_all | solution.py:19
  89.0 3.8 %reshape_reshape.3 = bf16[128,128,32]{2,1,0:T(8,128)(2,1)} reshape(bf16[32,4,4096]{2,1,0:T(4,128)(2,1)S(1)} %all-to-all-done.2) | data formatting | bytes 2097152 | tf_op jit(solution)/shard_map/reshape;reshape | solution.py:159
  92.8 4.0 %copy.104 = bf16[128,128,32,1]{1,0,3,2:T(8,128)(2,1)S(1)} copy(bf16[128,128,32,1]{2,1,0,3:T(8,128)(2,1)} %bitcast.145) | data formatting | bytes 2097152 | tf_op jit(solution)/shard_map/reshape;reshape | solution.py:159
  96.8 0.7 fusion.23
  97.5 0.7 copy.97
  98.3 1.1 %fusion.29 = bf16[4,128,128]{2,1,0:T(8,128)(2,1)} fusion(bf16[4,128,1024]{1,2,0:T(8,128)(2,1)S(1)} %bitcast.148, bf16[4,128,128]{2,1,0:T(8,128)(2,1)S(1)} %copy-done.2, bf16[1024,128]{1,0:T(8,128)(2,1)S(1)} %copy-done.4), kind=kOutput, calls=%fused_computation.39 | convolution fusion | flops 134414336 | bytes 1572864 | tf_op jit(solution)/shard_map/dot_general | solution.py:167
  (31 shorter events, 0.3 us)
Async XLA Ops:
  0.6 16.5 %copy-start = (bf16[256,1024]{1,0:T(8,128)(2,1)S(1)}, bf16[256,1024]{1,0:T(8,128)(2,1)}, u32[]{:S(2)}) copy-start(bf16[256,1024]{1,0:T(8,128)(2,1)} %param.14) | copy-start | bytes 1572868
  4.9 22.8 %all-to-all-start = ((bf16[32,8,4,128]{3,1,2,0:T(8,128)(2,1)}), bf16[32,8,4,128]{3,1,2,0:T(8,128)(2,1)S(1)}, u32[]{:S(2)}, u32[]{:S(2)}) async-start(bf16[32,8,4,128]{3,1,2,0:T(8,128)(2,1)} %broadcast_in_dim.12), calls=%async_computation | async-start | bytes 524288 | tf_op jit(solution)/shard_map/all_to_all | solution.py:19
  27.9 3.8 %copy-start.1 = (bf16[4,128,256]{2,1,0:T(8,128)(2,1)S(1)}, bf16[4,128,256]{2,1,0:T(8,128)(2,1)}, u32[]{:S(2)}) copy-start(bf16[4,128,256]{2,1,0:T(8,128)(2,1)} %param.11) | copy-start | bytes 786436
  27.9 3.8 %copy-start.5 = (bf16[256,256]{1,0:T(8,128)(2,1)S(1)}, bf16[256,256]{1,0:T(8,128)(2,1)}, u32[]{:S(2)}) copy-start(bf16[256,256]{1,0:T(8,128)(2,1)} %param.15) | copy-start | bytes 393220
  31.8 18.3 %copy-start.3 = (bf16[256,1024]{1,0:T(8,128)(2,1)S(1)}, bf16[256,1024]{1,0:T(8,128)(2,1)}, u32[]{:S(2)}) copy-start(bf16[256,1024]{1,0:T(8,128)(2,1)} %param.16) | copy-start | bytes 1572868
  53.8 2.0 %copy-start.6 = (bf16[256,256]{1,0:T(8,128)(2,1)S(1)}, bf16[256,256]{1,0:T(8,128)(2,1)}, u32[]{:S(2)}) copy-start(bf16[256,256]{1,0:T(8,128)(2,1)} %param.17) | copy-start | bytes 393220
  53.8 2.7 %copy-start.7 = (bf16[256,64]{0,1:T(8,128)(2,1)S(1)}, bf16[256,64]{0,1:T(8,128)(2,1)}, u32[]{:S(2)}) copy-start(bf16[256,64]{0,1:T(8,128)(2,1)} %param.18) | copy-start | bytes 98308
  58.7 30.4 %all-to-all-start.2 = ((bf16[32,4,4096]{2,1,0:T(4,128)(2,1)}), bf16[32,4,4096]{2,1,0:T(4,128)(2,1)S(1)}, u32[]{:S(2)}, u32[]{:S(2)}) async-start(bf16[32,4,4096]{2,1,0:T(4,128)(2,1)} %broadcast_in_dim.14), calls=%async_computation.2 | async-start | bytes 2097152 | tf_op jit(solution)/shard_map/all_to_all | solution.py:19
  96.8 1.4 %copy-start.2 = (bf16[4,128,128]{2,1,0:T(8,128)(2,1)S(1)}, bf16[4,128,128]{2,1,0:T(8,128)(2,1)}, u32[]{:S(2)}) copy-start(bf16[4,128,128]{2,1,0:T(8,128)(2,1)} %param.12) | copy-start | bytes 393220
  96.8 1.4 %copy-start.4 = (bf16[1024,128]{1,0:T(8,128)(2,1)S(1)}, bf16[1024,128]{1,0:T(8,128)(2,1)}, u32[]{:S(2)}) copy-start(bf16[1024,128]{1,0:T(8,128)(2,1)} %param.19) | copy-start | bytes 786436
where the time goes:
time: 100 us; the launch traced here: 99.4 us
  waiting for transfers between devices  33.7 us (34%)
  blocking collectives  16.2 us (16%)
  local copies, waits for them, and re-layouts  14.7 us (15%)
  matrix products  13.9 us (14%)
  starting transfers between devices  13.9 us (14%)
  other arithmetic  5.89 us (6%)
  between operations  1 us (1%)
    all_to_all x2, waiting for transfers between devices, copy_for_each(): lax.all_to_all(jnp.broadcast_to(array[None], (length, *array.shape)), axi...  33.7 us
    all_to_all x1, blocking collectives, per_device(): lax.all_to_all(alignment_blocks, 'dap', split_axis=1, concat_axis=0, tile...  16.2 us
    all_to_all x2, starting transfers between devices, copy_for_each(): lax.all_to_all(jnp.broadcast_to(array[None], (length, *array.shape)), axi...  13.9 us
    another operation x2, local copies, waits for them, and re-layouts, per_device(): right_three = segment.reshape(count_rows, homolog_tally, outer_width)  7.75 us
    sub x5, matrix products, attend(): expo = jnp.exp(scores - highest)  3.75 us
    reduce_sum x4, other arithmetic, standardize_features(): spread = jnp.mean(center * center, axis=-1, keepdims=True)  3.05 us
    dot_general x5, matrix products, attend(): jnp.einsum('bhij,bjhd->bihd', weights, value_rows, preferred_element_type...  3 us
    reduce_sum x3, other arithmetic, standardize_features(): center = values - jnp.mean(values, axis=-1, keepdims=True)  2.44 us
  transfers between devices with their start and end apart: 2, of which 2 were waited for; matrix products, arithmetic and copies ran while one was open for 5% of the time, Pallas kernels for 0%

commit v1 on v0

v1 whole, which is shorter than its diff:
```python
import math

import jax
import jax.numpy as jnp
from jax import lax
from jax.experimental import pallas as pl
from jax.experimental.pallas import tpu as pltpu
from jax.sharding import PartitionSpec as P

EPSILON = 1e-05
MESH = pl.DeviceIdType.MESH
F32 = jnp.float32
BF16 = jnp.bfloat16
LOG2E = math.log2(math.e)
NX = 4
NY = 8
ND = NX * NY
NT = (((1,), (1,)), ((), ()))


def standardized(values):
    center = values - jnp.mean(values, axis=-1, keepdims=True)
    spread = jnp.mean(center * center, axis=-1, keepdims=True)
    return center * lax.rsqrt(spread + EPSILON)


def dot(a, b):
    return jnp.dot(a, b, preferred_element_type=F32)


def dot_nt(a, b):
    return lax.dot_general(a, b, NT, preferred_element_type=F32)


def put(ref, start, size, value, stride=1):
    rows = pl.ds(start, size, stride=stride) if stride > 1 else pl.ds(start, size)
    for t in range(value.shape[1] // 128):
        ref[t, rows, :] = value[:, t * 128 : (t + 1) * 128]


def take(ref, start, size, stride):
    rows = pl.ds(start, size, stride=stride)
    return jnp.concatenate([ref[t, rows, :] for t in range(ref.shape[0])], axis=1)


def head_masks():
    lane = lax.broadcasted_iota(jnp.int32, (1, 128), 1)
    return [jnp.where(lane // 32 == h, 1.0, 0.0).astype(BF16) for h in range(4)]


def attend(q, k, v, gate, bias, masks):
    scale = LOG2E / math.sqrt(32)
    weights = []
    values = []
    for h in range(4):
        scores = dot_nt(q * masks[h], k) * scale
        if bias is not None:
            scores = scores + bias(h)
        highest = jnp.max(scores, axis=-1, keepdims=True)
        weights.append(jnp.exp2(scores - highest).astype(BF16))
        ones = jnp.broadcast_to(masks[h], v.shape)
        values.append(jnp.concatenate([v * masks[h], ones], axis=1))
    both = dot(jnp.concatenate(weights, axis=1), jnp.concatenate(values, axis=0))
    return (jax.nn.sigmoid(gate) * (both[:, :128] / both[:, 128:])).astype(BF16)


def kernel(
    hom,
    two,
    map_t,
    win,
    wout,
    cwin,
    cwout,
    fac_t,
    tpe,
    align_out,
    pair_out,
    hom_v,
    two_v,
    map_v,
    win_v,
    wout_v,
    cwin_v,
    cwout_v,
    fac_v,
    tpe_v,
    x32,
    n32,
    q_s,
    k_s,
    v_s,
    g_s,
    b32,
    bias_recv,
    bh,
    m32,
    msend,
    mrecv,
    y32,
    align_v,
    l_all,
    r_all,
    o32,
    ot,
    w32,
    bd,
    dsend,
    drecv,
    f32s,
    pair_v,
    in_sem,
    out_sem,
    bs_sem,
    br_sem,
    ms_sem,
    mr_sem,
    ls_sem,
    lr_sem,
    rs_sem,
    rr_sem,
    ds_sem,
    dr_sem,
):
    me = lax.axis_index("dap")
    y = me // NX
    x = lax.rem(me, NX)

    def remote(src, dst, send_sem, recv_sem, target):
        return pltpu.make_async_remote_copy(
            src_ref=src,
            dst_ref=dst,
            send_sem=send_sem,
            recv_sem=recv_sem,
            device_id={"dap": target},
            device_id_type=MESH,
        )

    pairs = [
        (two, two_v),
        (map_t, map_v),
        (hom, hom_v),
        (win, win_v),
        (tpe, tpe_v),
        (wout, wout_v),
        (cwin, cwin_v),
        (cwout, cwout_v),
        (fac_t, fac_v),
    ]
    loads = [pltpu.make_async_copy(a, b, in_sem.at[n]) for n, (a, b) in enumerate(pairs)]
    for load in loads:
        load.start()
    names = ("two", "map", "hom", "win", "tpe", "wout", "cwin", "cwout", "fac")
    ready = dict(zip(names, loads))

    barrier = pltpu.get_barrier_semaphore()

    def greet(step, carry):
        pl.semaphore_signal(
            barrier, inc=1, device_id={"dap": lax.rem(me + step, ND)}, device_id_type=MESH
        )
        return carry

    lax.fori_loop(1, ND, greet, 0)

    ready["two"].wait()
    ready["map"].wait()
    for i in range(4):
        pair_norm = standardized(two_v[i].astype(F32)).astype(BF16)
        b32[pl.ds(i, 8, stride=4), :] = dot_nt(map_v[...], pair_norm)
    bias_recv[me] = b32[0:32, :].astype(BF16)

    pl.semaphore_wait(barrier, ND - 1)

    y_order = [1, 7, 2, 6, 3, 5, 4]
    x_order = [1, 3, 2]
    bias_sends = []

    def send_bias(block, target):
        copy = remote(
            bias_recv.at[block],
            bias_recv.at[block],
            bs_sem.at[len(bias_sends)],
            br_sem.at[block],
            target,
        )
        copy.start()
        bias_sends.append(copy)

    def bias_arrived(block):
        remote(
            bias_recv.at[block], bias_recv.at[block], bs_sem.at[0], br_sem.at[block], me
        ).wait_recv()

    for k in reversed(y_order):
        send_bias(me, lax.rem(y + k, NY) * NX + x)
    for k in reversed(x_order):
        send_bias(me, y * NX + lax.rem(x + k, NX))

    ready["hom"].wait()
    ready["win"].wait()
    masks = head_masks()
    for s in range(4):
        values = hom_v[s].astype(F32)
        put(x32, s * 128, 128, values)
        normal = standardized(values)
        put(n32, s * 128, 128, normal)
        normal = normal.astype(BF16)
        k_s[s] = dot(normal, win_v[:, 256:512]).astype(BF16)
        v_s[s] = dot(normal, win_v[:, 512:768]).astype(BF16)

    def mixed(ref, s):
        return jnp.concatenate(
            [take(ref, s * 128 + i, 32, 4) for i in range(4)], axis=0
        )

    for s in range(4):
        normal = mixed(n32, s).astype(BF16)
        q_s[s] = dot(normal, win_v[:, 0:256]).astype(BF16)
        g_s[s] = dot(normal, win_v[:, 768:1024]).astype(BF16)

    ready["tpe"].wait()
    w32[...] = tpe_v[...].astype(F32)
    bd[...] = jnp.zeros_like(bd)
    for e in range(32):
        piece = w32[pl.ds(e, 32, stride=32), :].astype(BF16)
        for i in range(4):
            bd[e * 128 + i * 32 : e * 128 + (i + 1) * 32, i * 128 : (i + 1) * 128] = piece

    for k in y_order:
        block = lax.rem(y + k, NY) * NX + x
        bias_arrived(block)
        for m in x_order:
            send_bias(block, y * NX + lax.rem(x + m, NX))
    for k in [0] + y_order:
        for m in x_order:
            bias_arrived(lax.rem(y + k, NY) * NX + lax.rem(x + m, NX))

    b32[...] = bias_recv[...].reshape(ND * 32, 128).astype(F32) * LOG2E
    for h in range(8):
        for i in range(4):
            bh[h, i * 32 : (i + 1) * 32, :] = b32[pl.ds(h * 4 + i, 32, stride=32), :]

    ready["wout"].wait()
    for s in range(4):
        gated = []
        for g in range(2):
            lanes = slice(g * 128, (g + 1) * 128)
            gated.append(
                attend(
                    q_s[s, :, lanes],
                    k_s[s, :, lanes],
                    v_s[s, :, lanes],
                    g_s[s, :, lanes].astype(F32),
                    lambda h: bh[g * 4 + h],
                    masks,
                )
            )
        total = mixed(x32, s) + dot(jnp.concatenate(gated, axis=1), wout_v[...])
        put(m32, s * 128, 128, total)

    for d in range(ND):
        msend[d] = take(m32, d, 16, ND).astype(BF16)

    mrecv[me] = msend[me]

    def send_rows(step, carry):
        target = lax.rem(me + step, ND)
        remote(msend.at[target], mrecv.at[me], ms_sem, mr_sem, target).start()
        return carry

    lax.fori_loop(1, ND, send_rows, 0)

    for copy in bias_sends:
        copy.wait_send()
    for name in ("cwin", "cwout", "fac"):
        ready[name].wait()

    others = remote(
        msend.at[pl.ds(0, ND - 1)], mrecv.at[pl.ds(0, ND - 1)], ms_sem, mr_sem, me
    )
    others.wait_recv()
    others.wait_send()

    put(x32, 0, ND * 16, mrecv[...].reshape(ND * 16, 256).astype(F32))
    for r in range(4):
        values = take(x32, r, 128, 4)
        normal = standardized(values).astype(BF16)
        packed = [dot(normal, cwin_v[:, n * 256 : (n + 1) * 256]).astype(BF16) for n in range(4)]
        gated = []
        for g in range(2):
            lanes = slice(g * 128, (g + 1) * 128)
            q, k, v, gate = [part[:, lanes] for part in packed]
            gated.append(attend(q, k, v, gate.astype(F32), None, masks))
        total = (values + dot(jnp.concatenate(gated, axis=1), cwout_v[...])).astype(BF16)
        wide = total.astype(F32)
        put(y32, r, 128, wide, stride=4)
        outer_norm = standardized(wide).astype(BF16)
        factors = dot_nt(fac_v[...], outer_norm).astype(BF16)
        l_all[x, r * 32 : (r + 1) * 32, :] = factors[:32]
        r_all[y, r * 32 : (r + 1) * 32, :] = factors[32:]

    sends = []
    for n, k in enumerate(reversed(y_order)):
        target = lax.rem(y + k, NY) * NX + x
        sends.append(remote(r_all.at[y], r_all.at[y], rs_sem.at[n], rr_sem.at[y], target))
    for n, k in enumerate(reversed(x_order)):
        target = y * NX + lax.rem(x + k, NX)
        sends.append(remote(l_all.at[x], l_all.at[x], ls_sem.at[n], lr_sem.at[x], target))
    for copy in sends:
        copy.start()

    align_v[...] = jnp.concatenate([y32[0], y32[1]], axis=1).astype(BF16)
    align_store = pltpu.make_async_copy(align_v, align_out, out_sem.at[0])
    align_store.start()

    for k in x_order:
        peer = lax.rem(x + k, NX)
        remote(l_all.at[peer], l_all.at[peer], ls_sem.at[0], lr_sem.at[peer], me).wait_recv()
    left = l_all[...].reshape(NX * 128, 128)
    for k in [0] + y_order:
        peer = lax.rem(y + k, NY)
        if k:
            remote(r_all.at[peer], r_all.at[peer], rs_sem.at[0], rr_sem.at[peer], me).wait_recv()
        product = dot_nt(r_all[peer], left) * (1.0 / 128)
        put(o32, pl.multiple_of(peer * 128, 128), 128, product)
    for e in range(32):
        ot[:, e * 128 : (e + 1) * 128] = jnp.concatenate(
            [
                o32[n, pl.ds(j * 32 + e, 8, stride=128), :]
                for n in range(NX)
                for j in range(4)
            ],
            axis=0,
        ).astype(BF16)
    dsend[...] = dot(ot[...], bd[...]).astype(BF16).reshape(NX, 32, 512)
    drecv[x] = dsend[x]
    for n, k in enumerate(x_order):
        peer = lax.rem(x + k, NX)
        copy = remote(
            dsend.at[peer], drecv.at[x], ds_sem.at[n], dr_sem.at[x], y * NX + peer
        )
        copy.start()
        sends.append(copy)
    for k in x_order:
        peer = lax.rem(x + k, NX)
        remote(dsend.at[peer], drecv.at[peer], ds_sem.at[0], dr_sem.at[peer], me).wait_recv()
    for n in range(NX):
        block = drecv[n].astype(F32)
        for i in range(4):
            for j in range(4):
                f32s[pl.ds(i * 128 + n * 4 + j, 8, stride=16), :] = block[
                    j * 8 : (j + 1) * 8, i * 128 : (i + 1) * 128
                ]
    pair_v[...] = (f32s[...] + two_v[...].reshape(512, 128).astype(F32)).astype(BF16).reshape(4, 128, 128)
    pair_store = pltpu.make_async_copy(pair_v, pair_out, out_sem.at[1])
    pair_store.start()
    for copy in sends:
        copy.wait_send()
    align_store.wait()
    pair_store.wait()


def per_device(hom, two, offset_map, win, wout, cwin, cwout, factors, tpe):
    operands = (hom, two, offset_map.T, win, wout, cwin, cwout, factors.T, tpe)
    dma = pltpu.SemaphoreType.DMA
    vm = pltpu.VMEM
    scratch = [vm(a.shape, BF16) for a in operands] + [
        vm((2, 512, 128), F32),
        vm((2, 512, 128), F32),
        vm((4, 128, 256), BF16),
        vm((4, 128, 256), BF16),
        vm((4, 128, 256), BF16),
        vm((4, 128, 256), BF16),
        vm((ND * 32, 128), F32),
        vm((ND, 32, 128), BF16),
        vm((8, 128, 128), F32),
        vm((2, 512, 128), F32),
        vm((ND, 16, 256), BF16),
        vm((ND, 16, 256), BF16),
        vm((2, 512, 128), F32),
        vm((512, 256), BF16),
        vm((NX, 128, 128), BF16),
        vm((NY, 128, 128), BF16),
        vm((NX, NY * 128, 128), F32),
        vm((128, 4096), BF16),
        vm((1024, 128), F32),
        vm((4096, 512), BF16),
        vm((NX, 32, 512), BF16),
        vm((NX, 32, 512), BF16),
        vm((512, 128), F32),
        vm((4, 128, 128), BF16),
        dma((9,)),
        dma((2,)),
        dma((31,)),
        dma((ND,)),
        dma,
        dma,
        dma((3,)),
        dma((NX,)),
        dma((7,)),
        dma((NY,)),
        dma((3,)),
        dma((NX,)),
    ]
    hbm = pl.BlockSpec(memory_space=pl.ANY)
    align, pair = pl.pallas_call(
        kernel,
        out_shape=(
            jax.ShapeDtypeStruct((512, 256), BF16),
            jax.ShapeDtypeStruct((4, 128, 128), BF16),
        ),
        in_specs=[hbm] * len(operands),
        out_specs=(hbm, hbm),
        scratch_shapes=scratch,
        compiler_params=pltpu.CompilerParams(collective_id=0, has_side_effects=True),
    )(*operands)
    return align.reshape(128, 4, 256), pair


def solution(mesh):
    split = P(("crop", "dap"), None, None)
    return jax.shard_map(
        per_device,
        mesh=mesh,
        in_specs=(split, split) + (P(),) * 7,
        out_specs=(P("crop", "dap", None), split),
        check_vma=False,
    )
```

time: 100 us -> 51.8 us (0.52)
  Pallas kernels: 0 us -> 47.9 us
  waiting for transfers between devices: 33.7 us -> 0 us
  blocking collectives: 16.2 us -> 0 us
  matrix products: 13.9 us -> 0 us
  starting transfers between devices: 13.9 us -> 0 us
  local copies, waits for them, and re-layouts: 14.7 us -> 2.41 us
  other arithmetic: 5.89 us -> 0 us
    pallas_call x0 -> x1, Pallas kernels: none -> 47.9 us  [per_device(): pl.pallas_call(kernel, out_shape=(jax.ShapeDtypeStruct((512, 256), BF16),...]
    all_to_all x2 -> x0, waiting for transfers between devices: 33.7 us -> none  [copy_for_each(): lax.all_to_all(jnp.broadcast_to(array[None], (length, *array.shape)), axi...]
    all_to_all x1 -> x0, blocking collectives: 16.2 us -> none  [per_device(): lax.all_to_all(alignment_blocks, 'dap', split_axis=1, concat_axis=0, tile...]
    all_to_all x2 -> x0, starting transfers between devices: 13.9 us -> none  [copy_for_each(): lax.all_to_all(jnp.broadcast_to(array[None], (length, *array.shape)), axi...]
    dot_general x17 -> x0, matrix products: 10.2 us -> none  [the longest x5 3 us: attend(): jnp.einsum('bhij,bjhd->bihd', weights, value_rows, preferred_element_type...]
    another operation x2 -> x0, local copies, waits for them, and re-layouts: 7.75 us -> none  [per_device(): right_three = segment.reshape(count_rows, homolog_tally, outer_width)]
    reduce_sum x7 -> x0, other arithmetic: 5.49 us -> none  [the longest x4 3.05 us: standardize_features(): spread = jnp.mean(center * center, axis=-1, keepdims=True)]
    sub x5 -> x0, matrix products: 3.75 us -> none  [attend(): expo = jnp.exp(scores - highest)]
  transfers between devices with their start and end apart: 2 -> 0, of which waited for: 2 -> 0; matrix products, arithmetic and copies ran while one was open for 5% -> 0% of each run, Pallas kernels for 0% -> 0%
where the time goes in v1:
time: 51.8 us; the launch traced here: 50.9 us
  Pallas kernels  47.9 us (92%)
  local copies, waits for them, and re-layouts  2.41 us (5%)
  between operations  0.65 us (1%)
    pallas_call x1, Pallas kernels, per_device(): pl.pallas_call(kernel, out_shape=(jax.ShapeDtypeStruct((512, 256), BF16),...  47.9 us
    reshape x1, local copies, waits for them, and re-layouts, per_device(): return (align.reshape(128, 4, 256), pair)  1.75 us

profile of v1, /device:TPU:448, one launch (start us, length us, event | category | flops | bytes accessed | tf_op | source)
XLA Modules:
  0.0 50.9 jit_solution(17472028207866244313)
XLA Ops:
  0.6 47.9 %shard_map.104 = (bf16[512,256]{1,0:T(8,128)(2,1)}, bf16[4,128,128]{2,1,0:T(8,128)(2,1)}) custom-call(bf16[4,128,256]{2,1,0:T(8,128)(2,1)} %hom.1, bf16[4,128,128]{2,1,0:T(8,128)(2,1)} %two.1, bf16[8,128]{1,0:T(8,128)(2,1)} %bitcast.3, bf16[256,1024]{1,0:T(8,128)(2,1)} %win.1, bf16[256,256]{1,0:T(8,128)(2,1)} %wout.1, bf16[256,1024]{1,0:T(8,128)(2,1)} %cwin.1, ...), custom_call_target="tpu_custom_call" | custom-call | tf_op jit(solution)/shard_map/pallas_call | solution.py:407
  48.5 0.0 copy-start
  48.5 1.8 %reshape.7 = bf16[128,4,256]{2,1,0:T(4,128)(2,1)} reshape(bf16[512,256]{1,0:T(8,128)(2,1)} %get-tuple-element.4) | data formatting | bytes 524288 | tf_op jit(solution)/shard_map/reshape | solution.py:418
  50.3 0.0 copy-done
  50.3 0.7 %copy.12 = bf16[4,128,128]{2,1,0:T(8,128)(2,1)} copy(bf16[4,128,128]{2,1,0:T(8,128)(2,1)S(1)} %copy-done) | data formatting | bytes 262144
Async XLA Ops:
  48.5 1.8 %copy-start = (bf16[4,128,128]{2,1,0:T(8,128)(2,1)S(1)}, bf16[4,128,128]{2,1,0:T(8,128)(2,1)}, u32[]{:S(2)}) copy-start(bf16[4,128,128]{2,1,0:T(8,128)(2,1)} %get-tuple-element.9) | copy-start | bytes 393220

commit v2 on v1

v2 whole, which is shorter than its diff:
```python
import math

import jax
import jax.numpy as jnp
from jax import lax
from jax.experimental import pallas as pl
from jax.experimental.pallas import tpu as pltpu
from jax.sharding import PartitionSpec as P

EPSILON = 1e-05
MESH = pl.DeviceIdType.MESH
F32 = jnp.float32
BF16 = jnp.bfloat16
LOG2E = math.log2(math.e)
NX = 4
NY = 8
ND = NX * NY
NT = (((1,), (1,)), ((), ()))


def standardized(values):
    center = values - jnp.mean(values, axis=-1, keepdims=True)
    spread = jnp.mean(center * center, axis=-1, keepdims=True)
    return center * lax.rsqrt(spread + EPSILON)


def dot(a, b):
    return jnp.dot(a, b, preferred_element_type=F32)


def dot_nt(a, b):
    return lax.dot_general(a, b, NT, preferred_element_type=F32)


def put(ref, start, size, value, stride=1):
    rows = pl.ds(start, size, stride=stride) if stride > 1 else pl.ds(start, size)
    for t in range(value.shape[1] // 128):
        ref[t, rows, :] = value[:, t * 128 : (t + 1) * 128]


def take(ref, start, size, stride):
    rows = pl.ds(start, size, stride=stride)
    return jnp.concatenate([ref[t, rows, :] for t in range(ref.shape[0])], axis=1)


def head_masks():
    lane = lax.broadcasted_iota(jnp.int32, (1, 128), 1)
    return [jnp.where(lane // 32 == h, 1.0, 0.0).astype(BF16) for h in range(4)]


def attend(q, k, v, gate, masks):
    scale = LOG2E / math.sqrt(32)
    weights = []
    values = []
    for h in range(4):
        scores = dot_nt(q * masks[h], k) * scale
        highest = jnp.max(scores, axis=-1, keepdims=True)
        weights.append(jnp.exp2(scores - highest).astype(BF16))
        ones = jnp.broadcast_to(masks[h], v.shape)
        values.append(jnp.concatenate([v * masks[h], ones], axis=1))
    both = dot(jnp.concatenate(weights, axis=1), jnp.concatenate(values, axis=0))
    return (jax.nn.sigmoid(gate) * (both[:, :128] / both[:, 128:])).astype(BF16)


def kernel(
    hom,
    two,
    map_t,
    win,
    wout,
    cwin,
    cwout,
    fac_t,
    tpe,
    align_out,
    pair_out,
    hom_v,
    two_v,
    map_v,
    win_v,
    wout_v,
    cwin_v,
    cwout_v,
    fac_v,
    tpe_v,
    x32,
    n32,
    q_s,
    k_s,
    v_s,
    g_s,
    xp,
    b32,
    bias_recv,
    m32,
    msend,
    mrecv,
    y32,
    align_v,
    l_all,
    r_all,
    o32,
    ot,
    w32,
    bd,
    dsend,
    drecv,
    f32s,
    pair_v,
    in_sem,
    out_sem,
    bs_sem,
    br_sem,
    ms_sem,
    mr_sem,
    ls_sem,
    lr_sem,
    rs_sem,
    rr_sem,
    ds_sem,
    dr_sem,
):
    me = lax.axis_index("dap")
    y = me // NX
    x = lax.rem(me, NX)

    def remote(src, dst, send_sem, recv_sem, target):
        return pltpu.make_async_remote_copy(
            src_ref=src,
            dst_ref=dst,
            send_sem=send_sem,
            recv_sem=recv_sem,
            device_id={"dap": target},
            device_id_type=MESH,
        )

    pairs = [
        (two, two_v),
        (map_t, map_v),
        (hom, hom_v),
        (win, win_v),
        (tpe, tpe_v),
        (wout, wout_v),
        (cwin, cwin_v),
        (cwout, cwout_v),
        (fac_t, fac_v),
    ]
    loads = [pltpu.make_async_copy(a, b, in_sem.at[n]) for n, (a, b) in enumerate(pairs)]
    for load in loads:
        load.start()
    names = ("two", "map", "hom", "win", "tpe", "wout", "cwin", "cwout", "fac")
    ready = dict(zip(names, loads))

    barrier = pltpu.get_barrier_semaphore()

    y_order = [1, 7, 2, 6, 3, 5, 4]
    x_order = [1, 3, 2]

    def at(dy, dx):
        return lax.rem(y + dy, NY) * NX + lax.rem(x + dx, NX)

    for dy, dx in [(k, 0) for k in reversed(y_order)] + [(0, k) for k in reversed(x_order)]:
        pl.semaphore_signal(barrier, inc=1, device_id={"dap": at(dy, dx)}, device_id_type=MESH)

    ready["two"].wait()
    ready["map"].wait()
    for i in range(4):
        pair_norm = standardized(two_v[i].astype(F32)).astype(BF16)
        b32[0, pl.ds(i, 8, stride=4), :] = dot_nt(map_v[...], pair_norm)
    bias_recv[me] = b32[0, 0:32, :].astype(BF16)

    pl.semaphore_wait(barrier, NY + NX - 2)

    bias_sends = []

    def send_bias(block, target):
        copy = remote(
            bias_recv.at[block],
            bias_recv.at[block],
            bs_sem.at[len(bias_sends)],
            br_sem.at[block],
            target,
        )
        copy.start()
        bias_sends.append(copy)

    def bias_arrived(block):
        remote(
            bias_recv.at[block], bias_recv.at[block], bs_sem.at[0], br_sem.at[block], me
        ).wait_recv()

    for k in reversed(y_order):
        send_bias(me, at(k, 0))
    for k in reversed(x_order):
        send_bias(me, at(0, k))

    ready["hom"].wait()
    ready["win"].wait()
    masks = head_masks()
    wide_masks = [jnp.concatenate([mask, mask], axis=1).astype(F32) for mask in masks]
    values = hom_v[...].reshape(512, 256).astype(F32)
    put(x32, 0, 512, values)
    normal = standardized(values)
    put(n32, 0, 512, normal)
    normal = normal.astype(BF16)
    k_s[...] = dot(normal, win_v[:, 256:512]).astype(BF16)
    v_s[...] = dot(normal, win_v[:, 512:768]).astype(BF16)

    def mixed(ref, group):
        return jnp.concatenate(
            [take(ref, s * 128 + group * 4 + i, 8, 16) for s in range(4) for i in range(4)],
            axis=0,
        )

    normal = jnp.concatenate([mixed(n32, group) for group in range(NX)], axis=0).astype(BF16)
    q_s[...] = dot(normal, win_v[:, 0:256]).astype(BF16).reshape(NX, 128, 256)
    gates = dot(normal, win_v[:, 768:1024]).astype(BF16).astype(F32)
    g_s[...] = jax.nn.sigmoid(gates).reshape(NX, 128, 256)
    for group in range(NX):
        xp[group] = mixed(x32, group)

    ready["tpe"].wait()
    w32[...] = tpe_v[...].astype(F32)
    bd[...] = jnp.zeros_like(bd)
    for e in range(32):
        piece = w32[pl.ds(e, 32, stride=32), :].astype(BF16)
        for i in range(4):
            bd[e * 128 + i * 32 : e * 128 + (i + 1) * 32, i * 128 : (i + 1) * 128] = piece

    for k in y_order:
        block = at(k, 0)
        bias_arrived(block)
        for m in reversed(x_order):
            send_bias(block, at(0, m))

    ready["wout"].wait()
    scale = LOG2E / math.sqrt(32)
    ones = jnp.ones((128, 128), BF16)
    for n, m in enumerate([0] + x_order):
        column = lax.rem(x + m, NX)
        if m:
            for k in [0] + y_order:
                bias_arrived(at(k, m))
        for r in range(NY):
            b32[n, r * 32 : (r + 1) * 32, :] = bias_recv[r * NX + column].astype(F32) * LOG2E
        bias = [
            jnp.concatenate(
                [b32[n, pl.ds(g * 16 + i, 8, stride=32), :] for i in range(16)], axis=0
            )
            for g in range(2)
        ]
        parts = []
        for g in range(2):
            lanes = slice(g * 128, (g + 1) * 128)
            part = []
            for s in range(4):
                rows = slice(s * 32, (s + 1) * 32)
                query = q_s[column, rows, lanes]
                query = jnp.concatenate([query * mask for mask in masks], axis=0)
                scores = dot_nt(query, k_s[s * 128 : (s + 1) * 128, lanes]) * scale + bias[g]
                highest = jnp.max(scores, axis=-1, keepdims=True)
                weights = jnp.exp2(scores - highest).astype(BF16)
                value = jnp.concatenate([v_s[s * 128 : (s + 1) * 128, lanes], ones], axis=1)
                both = dot(weights, value)
                both = sum(
                    both[h * 32 : (h + 1) * 32] * wide_masks[h] for h in range(4)
                )
                part.append(both[:, :128] / both[:, 128:] * g_s[column, rows, lanes])
            parts.append(jnp.concatenate(part, axis=0).astype(BF16))
        total = xp[column] + dot(jnp.concatenate(parts, axis=1), wout_v[...])
        put(m32.at[n], 0, 128, total)
        for r in range(NY):
            msend[r * NX + column] = take(m32.at[n], r, 16, 8).astype(BF16)
        if not m:
            mrecv[me] = msend[me]
        for k in ([] if m == 0 else [0]) + y_order:
            target = at(k, m)
            remote(msend.at[target], mrecv.at[me], ms_sem, mr_sem, target).start()

    for copy in bias_sends:
        copy.wait_send()
    for name in ("cwin", "cwout", "fac"):
        ready[name].wait()

    others = remote(
        msend.at[pl.ds(0, ND - 1)], mrecv.at[pl.ds(0, ND - 1)], ms_sem, mr_sem, me
    )
    others.wait_recv()
    others.wait_send()

    put(x32, 0, ND * 16, mrecv[...].reshape(ND * 16, 256).astype(F32))
    sends = []
    for half in range(2):
        pair = (half * 2, half * 2 + 1)
        values = jnp.concatenate([take(x32, r, 128, 4) for r in pair], axis=0)
        normal = standardized(values).astype(BF16)
        packed = [dot(normal, cwin_v[:, n * 256 : (n + 1) * 256]).astype(BF16) for n in range(4)]
        gated = []
        for n in range(2):
            parts = []
            for g in range(2):
                q, k, v, gate = [
                    part[n * 128 : (n + 1) * 128, g * 128 : (g + 1) * 128] for part in packed
                ]
                parts.append(attend(q, k, v, gate.astype(F32), masks))
            gated.append(jnp.concatenate(parts, axis=1))
        total = values + dot(jnp.concatenate(gated, axis=0), cwout_v[...])
        wide = total.astype(BF16).astype(F32)
        factors = dot_nt(fac_v[...], standardized(wide).astype(BF16)).astype(BF16)
        for n, r in enumerate(pair):
            l_all[x, r * 32 : (r + 1) * 32, :] = factors[:32, n * 128 : (n + 1) * 128]
            r_all[y, r * 32 : (r + 1) * 32, :] = factors[32:, n * 128 : (n + 1) * 128]
        for n, r in enumerate(pair):
            put(y32, r, 128, wide[n * 128 : (n + 1) * 128], stride=4)
        rows = pl.ds(half * 64, 64)
        start = len(sends)
        for n, k in enumerate(reversed(y_order)):
            block = r_all.at[y, rows]
            sends.append(
                remote(block, block, rs_sem.at[half, n], rr_sem.at[half, y], at(k, 0))
            )
        for n, k in enumerate(reversed(x_order)):
            block = l_all.at[x, rows]
            sends.append(
                remote(block, block, ls_sem.at[half, n], lr_sem.at[half, x], at(0, k))
            )
        for copy in sends[start:]:
            copy.start()

    align_v[...] = jnp.concatenate([y32[0], y32[1]], axis=1).reshape(128, 4, 256).astype(BF16)
    align_store = pltpu.make_async_copy(align_v, align_out, out_sem.at[0])
    align_store.start()

    def arrived(ref, peer, send_sem, recv_sem):
        for half in range(2):
            block = ref.at[peer, pl.ds(half * 64, 64)]
            remote(block, block, send_sem.at[half, 0], recv_sem.at[half, peer], me).wait_recv()

    for k in x_order:
        arrived(l_all, lax.rem(x + k, NX), ls_sem, lr_sem)
    left = l_all[...].reshape(NX * 128, 128)
    for k in [0] + y_order:
        peer = lax.rem(y + k, NY)
        if k:
            arrived(r_all, peer, rs_sem, rr_sem)
        product = dot_nt(r_all[peer], left) * (1.0 / 128)
        put(o32, pl.multiple_of(peer * 128, 128), 128, product)
    for e in range(32):
        ot[:, e * 128 : (e + 1) * 128] = jnp.concatenate(
            [
                o32[n, pl.ds(j * 32 + e, 8, stride=128), :]
                for n in range(NX)
                for j in range(4)
            ],
            axis=0,
        ).astype(BF16)
    for half in range(2):
        product = dot(ot[...], bd[:, half * 256 : (half + 1) * 256])
        dsend[half] = product.astype(BF16).reshape(NX, 32, 256)
        for n, k in enumerate(reversed(x_order)):
            peer = lax.rem(x + k, NX)
            copy = remote(
                dsend.at[half, peer],
                drecv.at[half, x],
                ds_sem.at[half, n],
                dr_sem.at[half, x],
                at(0, k),
            )
            copy.start()
            sends.append(copy)
    drecv[:, x] = dsend[:, x]
    for k in [0] + x_order:
        peer = lax.rem(x + k, NX)
        for half in range(2):
            if k:
                block = drecv.at[half, peer]
                remote(
                    block, block, ds_sem.at[half, 0], dr_sem.at[half, peer], me
                ).wait_recv()
            block = drecv[half, peer].astype(F32)
            for i in range(2):
                for j in range(4):
                    f32s[pl.ds((half * 2 + i) * 128 + peer * 4 + j, 8, stride=16), :] = block[
                        j * 8 : (j + 1) * 8, i * 128 : (i + 1) * 128
                    ]
    pair_v[...] = (f32s[...] + two_v[...].reshape(512, 128).astype(F32)).astype(BF16).reshape(4, 128, 128)
    pair_store = pltpu.make_async_copy(pair_v, pair_out, out_sem.at[1])
    pair_store.start()
    for copy in sends:
        copy.wait_send()
    align_store.wait()
    pair_store.wait()


def per_device(hom, two, offset_map, win, wout, cwin, cwout, factors, tpe):
    operands = (hom, two, offset_map.T, win, wout, cwin, cwout, factors.T, tpe)
    dma = pltpu.SemaphoreType.DMA
    vm = pltpu.VMEM
    scratch = [vm(a.shape, BF16) for a in operands] + [
        vm((2, 512, 128), F32),
        vm((2, 512, 128), F32),
        vm((NX, 128, 256), BF16),
        vm((512, 256), BF16),
        vm((512, 256), BF16),
        vm((NX, 128, 256), F32),
        vm((NX, 128, 256), F32),
        vm((NX, 256, 128), F32),
        vm((ND, 32, 128), BF16),
        vm((NX, 2, 128, 128), F32),
        vm((ND, 16, 256), BF16),
        vm((ND, 16, 256), BF16),
        vm((2, 512, 128), F32),
        vm((128, 4, 256), BF16),
        vm((NX, 128, 128), BF16),
        vm((NY, 128, 128), BF16),
        vm((NX, NY * 128, 128), F32),
        vm((128, 4096), BF16),
        vm((1024, 128), F32),
        vm((4096, 512), BF16),
        vm((2, NX, 32, 256), BF16),
        vm((2, NX, 32, 256), BF16),
        vm((512, 128), F32),
        vm((4, 128, 128), BF16),
        dma((9,)),
        dma((2,)),
        dma((31,)),
        dma((ND,)),
        dma,
        dma,
        dma((2, 3)),
        dma((2, NX)),
        dma((2, 7)),
        dma((2, NY)),
        dma((2, 3)),
        dma((2, NX)),
    ]
    hbm = pl.BlockSpec(memory_space=pl.ANY)
    align, pair = pl.pallas_call(
        kernel,
        out_shape=(
            jax.ShapeDtypeStruct((128, 4, 256), BF16),
            jax.ShapeDtypeStruct((4, 128, 128), BF16),
        ),
        in_specs=[hbm] * len(operands),
        out_specs=(hbm, hbm),
        scratch_shapes=scratch,
        compiler_params=pltpu.CompilerParams(collective_id=0, has_side_effects=True),
    )(*operands)
    return align, pair


def solution(mesh):
    split = P(("crop", "dap"), None, None)
    return jax.shard_map(
        per_device,
        mesh=mesh,
        in_specs=(split, split) + (P(),) * 7,
        out_specs=(P("crop", "dap", None), split),
        check_vma=False,
    )
```

time: 51.8 us -> 45.7 us (0.88)
  Pallas kernels: 47.9 us -> 42 us
    pallas_call x1, Pallas kernels: 47.9 us -> 42 us  [per_device(): pl.pallas_call(kernel, out_shape=(jax.ShapeDtypeStruct((128, 4, 256), BF1...]
    unnamed x3 -> x4, local copies, waits for them, and re-layouts: 0.66 us -> 2.44 us
    reshape x1 -> x0, local copies, waits for them, and re-layouts: 1.75 us -> none  [per_device(): return (align.reshape(128, 4, 256), pair)]
where the time goes in v2:
time: 45.7 us; the launch traced here: 45.1 us
  Pallas kernels  42 us (92%)
  local copies, waits for them, and re-layouts  2.44 us (5%)
  between operations  0.65 us (1%)
    pallas_call x1, Pallas kernels, per_device(): pl.pallas_call(kernel, out_shape=(jax.ShapeDtypeStruct((128, 4, 256), BF1...  42 us
    unnamed x4, local copies, waits for them, and re-layouts  2.44 us

profile of v2, /device:TPU:448, one launch (start us, length us, event | category | flops | bytes accessed | tf_op | source)
XLA Modules:
  0.0 45.1 jit_solution(18344383059209639791)
XLA Ops:
  0.6 42.0 %shard_map.104 = (bf16[128,4,256]{2,1,0:T(4,128)(2,1)}, bf16[4,128,128]{2,1,0:T(8,128)(2,1)}) custom-call(bf16[4,128,256]{2,1,0:T(8,128)(2,1)} %hom.1, bf16[4,128,128]{2,1,0:T(8,128)(2,1)} %two.1, bf16[8,128]{1,0:T(8,128)(2,1)} %bitcast.3, bf16[256,1024]{1,0:T(8,128)(2,1)} %win.1, bf16[256,256]{1,0:T(8,128)(2,1)} %wout.1, bf16[256,1024]{1,0:T(8,128)(2,1)} %cwin.1, ...), custom_call_target="tpu_custom_call" | custom-call | tf_op jit(solution)/shard_map/pallas_call | solution.py:438
  42.7 0.0 copy-start
  42.7 1.8 %copy.13 = bf16[128,4,256]{2,1,0:T(4,128)(2,1)} copy(bf16[128,4,256]{2,1,0:T(4,128)(2,1)} %get-tuple-element.4) | data formatting | bytes 524288
  44.4 0.0 copy-done
  44.4 0.7 %copy.14 = bf16[4,128,128]{2,1,0:T(8,128)(2,1)} copy(bf16[4,128,128]{2,1,0:T(8,128)(2,1)S(1)} %copy-done) | data formatting | bytes 262144
Async XLA Ops:
  42.7 1.8 %copy-start = (bf16[4,128,128]{2,1,0:T(8,128)(2,1)S(1)}, bf16[4,128,128]{2,1,0:T(8,128)(2,1)}, u32[]{:S(2)}) copy-start(bf16[4,128,128]{2,1,0:T(8,128)(2,1)} %get-tuple-element.5) | copy-start | bytes 393220

commit v3 on v2

--- a/solution.py
+++ b/solution.py
@@ -96,7 +96,6 @@
     msend,
     mrecv,
     y32,
-    align_v,
     l_all,
     r_all,
     o32,
@@ -106,9 +105,7 @@
     dsend,
     drecv,
     f32s,
-    pair_v,
     in_sem,
-    out_sem,
     bs_sem,
     br_sem,
     ms_sem,
@@ -236,7 +233,7 @@
     ready["wout"].wait()
     scale = LOG2E / math.sqrt(32)
     ones = jnp.ones((128, 128), BF16)
-    for n, m in enumerate([0] + x_order):
+    for n, m in enumerate([0, 1, 2, 3]):
         column = lax.rem(x + m, NX)
         if m:
             for k in [0] + y_order:
@@ -268,32 +265,57 @@
                 part.append(both[:, :128] / both[:, 128:] * g_s[column, rows, lanes])
             parts.append(jnp.concatenate(part, axis=0).astype(BF16))
         total = xp[column] + dot(jnp.concatenate(parts, axis=1), wout_v[...])
-        put(m32.at[n], 0, 128, total)
+        for s in range(4):
+            for i in range(4):
+                start = s * 32 + i * 8
+                for t in range(2):
+                    m32[n, t, pl.ds(i * 4 + s, 8, stride=16), :] = total[
+                        start : start + 8, t * 128 : (t + 1) * 128
+                    ]
         for r in range(NY):
-            msend[r * NX + column] = take(m32.at[n], r, 16, 8).astype(BF16)
+            rows = slice(r * 16, (r + 1) * 16)
+            msend[r * NX + column] = jnp.concatenate(
+                [m32[n, 0, rows, :], m32[n, 1, rows, :]], axis=1
+            ).astype(BF16)
         if not m:
             mrecv[me] = msend[me]
-        for k in ([] if m == 0 else [0]) + y_order:
+        for k in list(reversed(y_order)) + ([] if m == 0 else [0]):
             target = at(k, m)
-            remote(msend.at[target], mrecv.at[me], ms_sem, mr_sem, target).start()
+            remote(msend.at[target], mrecv.at[me], ms_sem, mr_sem.at[m], target).start()
 
     for copy in bias_sends:
         copy.wait_send()
     for name in ("cwin", "cwout", "fac"):
         ready[name].wait()
 
-    others = remote(
-        msend.at[pl.ds(0, ND - 1)], mrecv.at[pl.ds(0, ND - 1)], ms_sem, mr_sem, me
-    )
-    others.wait_recv()
-    others.wait_send()
-
-    put(x32, 0, ND * 16, mrecv[...].reshape(ND * 16, 256).astype(F32))
+    for m in range(NX):
+        column = lax.rem(x + NX - m, NX)
+        count = NY - 1 if m == 0 else NY
+        group = mrecv.at[pl.ds(0, count)]
+        remote(group, group, ms_sem, mr_sem.at[m], me).wait_recv()
+        values = jnp.concatenate([mrecv[r * NX + column] for r in range(NY)], axis=0).astype(F32)
+        normal = standardized(values)
+        base = pl.multiple_of(column * 32, 32)
+        for r in range(NY):
+            for i in range(4):
+                start = r * 16 + i * 4
+                for t in range(2):
+                    lanes = slice(t * 128, (t + 1) * 128)
+                    x32.at[t, pl.ds(i * 128 + base, 32), :][r * 4 : (r + 1) * 4, :] = values[
+                        start : start + 4, lanes
+                    ]
+                    n32.at[t, pl.ds(i * 128 + base, 32), :][r * 4 : (r + 1) * 4, :] = normal[
+                        start : start + 4, lanes
+                    ]
+    everything = msend.at[pl.ds(0, ND - 1)]
+    remote(everything, everything, ms_sem, mr_sem.at[0], me).wait_send()
+
     sends = []
     for half in range(2):
         pair = (half * 2, half * 2 + 1)
-        values = jnp.concatenate([take(x32, r, 128, 4) for r in pair], axis=0)
-        normal = standardized(values).astype(BF16)
+        rows = slice(half * 256, (half + 1) * 256)
+        values = jnp.concatenate([x32[0, rows, :], x32[1, rows, :]], axis=1)
+        normal = jnp.concatenate([n32[0, rows, :], n32[1, rows, :]], axis=1).astype(BF16)
         packed = [dot(normal, cwin_v[:, n * 256 : (n + 1) * 256]).astype(BF16) for n in range(4)]
         gated = []
         for n in range(2):
@@ -310,8 +332,6 @@
         for n, r in enumerate(pair):
             l_all[x, r * 32 : (r + 1) * 32, :] = factors[:32, n * 128 : (n + 1) * 128]
             r_all[y, r * 32 : (r + 1) * 32, :] = factors[32:, n * 128 : (n + 1) * 128]
-        for n, r in enumerate(pair):
-            put(y32, r, 128, wide[n * 128 : (n + 1) * 128], stride=4)
         rows = pl.ds(half * 64, 64)
         start = len(sends)
         for n, k in enumerate(reversed(y_order)):
@@ -326,33 +346,39 @@
             )
         for copy in sends[start:]:
             copy.start()
-
-    align_v[...] = jnp.concatenate([y32[0], y32[1]], axis=1).reshape(128, 4, 256).astype(BF16)
-    align_store = pltpu.make_async_copy(align_v, align_out, out_sem.at[0])
-    align_store.start()
-
-    def arrived(ref, peer, send_sem, recv_sem):
-        for half in range(2):
-            block = ref.at[peer, pl.ds(half * 64, 64)]
-            remote(block, block, send_sem.at[half, 0], recv_sem.at[half, peer], me).wait_recv()
-
-    for k in x_order:
-        arrived(l_all, lax.rem(x + k, NX), ls_sem, lr_sem)
+        for n, r in enumerate(pair):
+            for c in range(NX):
+                for d in range(NY):
+                    begin = n * 128 + c * 32 + d * 4
+                    put(y32, (d * NX + c) * 16 + r, 4, wide[begin : begin + 4], stride=4)
+
+    align_out[...] = jnp.concatenate([y32[0], y32[1]], axis=1).reshape(128, 4, 256).astype(BF16)
+
+    def arrived(ref, peer, half, send_sem, recv_sem):
+        block = ref.at[peer, pl.ds(half * 64, 64)]
+        remote(block, block, send_sem.at[half, 0], recv_sem.at[half, peer], me).wait_recv()
+
+    for half in range(2):
+        for k in x_order:
+            arrived(l_all, lax.rem(x + k, NX), half, ls_sem, lr_sem)
     left = l_all[...].reshape(NX * 128, 128)
-    for k in [0] + y_order:
-        peer = lax.rem(y + k, NY)
-        if k:
-            arrived(r_all, peer, rs_sem, rr_sem)
-        product = dot_nt(r_all[peer], left) * (1.0 / 128)
-        put(o32, pl.multiple_of(peer * 128, 128), 128, product)
+    for half in range(2):
+        for k in [0] + y_order:
+            peer = lax.rem(y + k, NY)
+            if k:
+                arrived(r_all, peer, half, rs_sem, rr_sem)
+            right = r_all[peer, half * 64 : (half + 1) * 64, :]
+            product = dot_nt(right, left) * (1.0 / 128)
+            for j in range(2):
+                for e in range(0, 32, 8):
+                    for n in range(NX):
+                        start = e * 32 + (half * 2 + j) * 8 + peer
+                        o32[n, pl.ds(start, 8, stride=32), :] = product[
+                            j * 32 + e : j * 32 + e + 8, n * 128 : (n + 1) * 128
+                        ]
     for e in range(32):
         ot[:, e * 128 : (e + 1) * 128] = jnp.concatenate(
-            [
-                o32[n, pl.ds(j * 32 + e, 8, stride=128), :]
-                for n in range(NX)
-                for j in range(4)
-            ],
-            axis=0,
+            [o32[n, e * 32 : (e + 1) * 32, :] for n in range(NX)], axis=0
         ).astype(BF16)
     for half in range(2):
         product = dot(ot[...], bd[:, half * 256 : (half + 1) * 256])
@@ -383,17 +409,14 @@
                     f32s[pl.ds((half * 2 + i) * 128 + peer * 4 + j, 8, stride=16), :] = block[
                         j * 8 : (j + 1) * 8, i * 128 : (i + 1) * 128
                     ]
-    pair_v[...] = (f32s[...] + two_v[...].reshape(512, 128).astype(F32)).astype(BF16).reshape(4, 128, 128)
-    pair_store = pltpu.make_async_copy(pair_v, pair_out, out_sem.at[1])
-    pair_store.start()
+    pair_out[...] = (f32s[...] + two_v[...].reshape(512, 128).astype(F32)).astype(BF16).reshape(4, 128, 128)
     for copy in sends:
         copy.wait_send()
-    align_store.wait()
-    pair_store.wait()
 
 
 def per_device(hom, two, offset_map, win, wout, cwin, cwout, factors, tpe):
     operands = (hom, two, offset_map.T, win, wout, cwin, cwout, factors.T, tpe)
+    operands = tuple(pltpu.with_memory_space_constraint(a, pltpu.HBM) for a in operands)
     dma = pltpu.SemaphoreType.DMA
     vm = pltpu.VMEM
     scratch = [vm(a.shape, BF16) for a in operands] + [
@@ -410,7 +433,6 @@
         vm((ND, 16, 256), BF16),
         vm((ND, 16, 256), BF16),
         vm((2, 512, 128), F32),
-        vm((128, 4, 256), BF16),
         vm((NX, 128, 128), BF16),
         vm((NY, 128, 128), BF16),
         vm((NX, NY * 128, 128), F32),
@@ -420,13 +442,11 @@
         vm((2, NX, 32, 256), BF16),
         vm((2, NX, 32, 256), BF16),
         vm((512, 128), F32),
-        vm((4, 128, 128), BF16),
         dma((9,)),
-        dma((2,)),
         dma((31,)),
         dma((ND,)),
         dma,
-        dma,
+        dma((NX,)),
         dma((2, 3)),
         dma((2, NX)),
         dma((2, 7)),
@@ -442,9 +462,9 @@
             jax.ShapeDtypeStruct((4, 128, 128), BF16),
         ),
         in_specs=[hbm] * len(operands),
-        out_specs=(hbm, hbm),
+        out_specs=(pl.BlockSpec(memory_space=pltpu.VMEM),) * 2,
         scratch_shapes=scratch,
-        compiler_params=pltpu.CompilerParams(collective_id=0, has_side_effects=True),
+        compiler_params=pltpu.CompilerParams(collective_id=0, has_side_effects=True, vmem_limit_bytes=40 * 2**20),
     )(*operands)
     return align, pair
 

time: 45.7 us -> 44.2 us (0.967)
  local copies, waits for them, and re-layouts: 2.44 us -> 1.36 us
    unnamed x4 -> x2, local copies, waits for them, and re-layouts: 2.44 us -> 1.36 us
where the time goes in v3:
time: 44.2 us; the launch traced here: 44 us
  Pallas kernels  42 us (95%)
  local copies, waits for them, and re-layouts  1.36 us (3%)
  between operations  0.64 us (1%)
    pallas_call x1, Pallas kernels, per_device(): pl.pallas_call(kernel, out_shape=(jax.ShapeDtypeStruct((128, 4, 256), BF1...  42 us
    unnamed x2, local copies, waits for them, and re-layouts  1.36 us

profile of v3, /device:TPU:448, one launch (start us, length us, event | category | flops | bytes accessed | tf_op | source)
XLA Modules:
  0.0 44.0 jit_solution(510974549652106823)
XLA Ops:
  0.6 42.0 %shard_map.104 = (bf16[128,4,256]{2,1,0:T(4,128)(2,1)S(1)}, bf16[4,128,128]{2,1,0:T(8,128)(2,1)S(1)}) custom-call(bf16[4,128,256]{2,1,0:T(8,128)(2,1)} %hom.1, bf16[4,128,128]{2,1,0:T(8,128)(2,1)} %two.1, bf16[8,128]{1,0:T(8,128)(2,1)} %bitcast.3, bf16[256,1024]{1,0:T(8,128)(2,1)} %win.1, bf16[256,256]{1,0:T(8,128)(2,1)} %wout.1, bf16[256,1024]{1,0:T(8,128)(2,1)} %cwin.1, ...), custom_call_target="tpu_custom_call" | custom-call | tf_op jit(solution)/shard_map/pallas_call | solution.py:458
  42.7 0.7 %copy.13 = bf16[128,4,256]{2,1,0:T(4,128)(2,1)} copy(bf16[128,4,256]{2,1,0:T(4,128)(2,1)S(1)} %get-tuple-element.4) | data formatting | bytes 524288
  43.4 0.7 %copy.14 = bf16[4,128,128]{2,1,0:T(8,128)(2,1)} copy(bf16[4,128,128]{2,1,0:T(8,128)(2,1)S(1)} %get-tuple-element.5) | data formatting | bytes 262144

commit v4 on v3

--- a/solution.py
+++ b/solution.py
@@ -188,7 +188,7 @@
 
     for k in reversed(y_order):
         send_bias(me, at(k, 0))
-    for k in reversed(x_order):
+    for k in (1, 3):
         send_bias(me, at(0, k))
 
     ready["hom"].wait()
@@ -227,15 +227,20 @@
     for k in y_order:
         block = at(k, 0)
         bias_arrived(block)
-        for m in reversed(x_order):
+        for m in (1, 3):
             send_bias(block, at(0, m))
 
     ready["wout"].wait()
     scale = LOG2E / math.sqrt(32)
     ones = jnp.ones((128, 128), BF16)
-    for n, m in enumerate([0, 1, 2, 3]):
+    for n, m in enumerate([0, 1, 3, 2]):
         column = lax.rem(x + m, NX)
-        if m:
+        if m == 1:
+            for k in [0] + y_order:
+                for dx in (1, 3):
+                    bias_arrived(at(k, dx))
+                send_bias(at(k, 1 if k % 2 else 3), at(0, 3 if k % 2 else 1))
+        if m == 2:
             for k in [0] + y_order:
                 bias_arrived(at(k, m))
         for r in range(NY):
@@ -310,7 +315,29 @@
     everything = msend.at[pl.ds(0, ND - 1)]
     remote(everything, everything, ms_sem, mr_sem.at[0], me).wait_send()
 
+    def arrived(ref, peer, half, send_sem, recv_sem):
+        block = ref.at[peer, pl.ds(half * 64, 64)]
+        remote(block, block, send_sem.at[half, 0], recv_sem.at[half, peer], me).wait_recv()
+
     sends = []
+
+    def pass_on(half):
+        slot = 4
+        for k in (2, 6):
+            peer = lax.rem(y + k, NY)
+            arrived(r_all, peer, half, rs_sem, rr_sem)
+            block = r_all.at[peer, pl.ds(half * 64, 64)]
+            targets = [1 if k == 6 else 7]
+            if (k == 6) == (half == 0):
+                targets = [2 if k == 6 else 6] + targets
+            for target in targets:
+                copy = remote(
+                    block, block, rs_sem.at[half, slot], rr_sem.at[half, peer], at(target, 0)
+                )
+                copy.start()
+                sends.append(copy)
+                slot += 1
+
     for half in range(2):
         pair = (half * 2, half * 2 + 1)
         rows = slice(half * 256, (half + 1) * 256)
@@ -334,7 +361,7 @@
             r_all[y, r * 32 : (r + 1) * 32, :] = factors[32:, n * 128 : (n + 1) * 128]
         rows = pl.ds(half * 64, 64)
         start = len(sends)
-        for n, k in enumerate(reversed(y_order)):
+        for n, k in enumerate((2, 6, 1, 7)):
             block = r_all.at[y, rows]
             sends.append(
                 remote(block, block, rs_sem.at[half, n], rr_sem.at[half, y], at(k, 0))
@@ -346,6 +373,8 @@
             )
         for copy in sends[start:]:
             copy.start()
+        if half:
+            pass_on(0)
         for n, r in enumerate(pair):
             for c in range(NX):
                 for d in range(NY):
@@ -354,10 +383,7 @@
 
     align_out[...] = jnp.concatenate([y32[0], y32[1]], axis=1).reshape(128, 4, 256).astype(BF16)
 
-    def arrived(ref, peer, half, send_sem, recv_sem):
-        block = ref.at[peer, pl.ds(half * 64, 64)]
-        remote(block, block, send_sem.at[half, 0], recv_sem.at[half, peer], me).wait_recv()
-
+    pass_on(1)
     for half in range(2):
         for k in x_order:
             arrived(l_all, lax.rem(x + k, NX), half, ls_sem, lr_sem)
@@ -365,7 +391,7 @@
     for half in range(2):
         for k in [0] + y_order:
             peer = lax.rem(y + k, NY)
-            if k:
+            if k not in (0, 2, 6):
                 arrived(r_all, peer, half, rs_sem, rr_sem)
             right = r_all[peer, half * 64 : (half + 1) * 64, :]
             product = dot_nt(right, left) * (1.0 / 128)

time: 44.2 us -> 46.7 us (1.057)
  Pallas kernels: 42 us -> 44.1 us
    pallas_call x1, Pallas kernels: 42 us -> 44.1 us  [per_device(): pl.pallas_call(kernel, out_shape=(jax.ShapeDtypeStruct((128, 4, 256), BF1...]
where the time goes in v4:
time: 46.7 us; the launch traced here: 46.1 us
  Pallas kernels  44.1 us (94%)
  local copies, waits for them, and re-layouts  1.36 us (3%)
  between operations  0.64 us (1%)
    pallas_call x1, Pallas kernels, per_device(): pl.pallas_call(kernel, out_shape=(jax.ShapeDtypeStruct((128, 4, 256), BF1...  44.1 us
    unnamed x2, local copies, waits for them, and re-layouts  1.36 us

profile of v4, /device:TPU:448, one launch (start us, length us, event | category | flops | bytes accessed | tf_op | source)
XLA Modules:
  0.0 46.1 jit_solution(5252746265002775134)
XLA Ops:
  0.6 44.1 %shard_map.104 = (bf16[128,4,256]{2,1,0:T(4,128)(2,1)S(1)}, bf16[4,128,128]{2,1,0:T(8,128)(2,1)S(1)}) custom-call(bf16[4,128,256]{2,1,0:T(8,128)(2,1)} %hom.1, bf16[4,128,128]{2,1,0:T(8,128)(2,1)} %two.1, bf16[8,128]{1,0:T(8,128)(2,1)} %bitcast.3, bf16[256,1024]{1,0:T(8,128)(2,1)} %win.1, bf16[256,256]{1,0:T(8,128)(2,1)} %wout.1, bf16[256,1024]{1,0:T(8,128)(2,1)} %cwin.1, ...), custom_call_target="tpu_custom_call" | custom-call | tf_op jit(solution)/shard_map/pallas_call | solution.py:484
  44.7 0.7 %copy.13 = bf16[128,4,256]{2,1,0:T(4,128)(2,1)} copy(bf16[128,4,256]{2,1,0:T(4,128)(2,1)S(1)} %get-tuple-element.4) | data formatting | bytes 524288
  45.5 0.7 %copy.14 = bf16[4,128,128]{2,1,0:T(8,128)(2,1)} copy(bf16[4,128,128]{2,1,0:T(8,128)(2,1)S(1)} %get-tuple-element.5) | data formatting | bytes 262144

commit v5 on v3

--- a/solution.py
+++ b/solution.py
@@ -380,38 +380,38 @@
         ot[:, e * 128 : (e + 1) * 128] = jnp.concatenate(
             [o32[n, e * 32 : (e + 1) * 32, :] for n in range(NX)], axis=0
         ).astype(BF16)
-    for half in range(2):
-        product = dot(ot[...], bd[:, half * 256 : (half + 1) * 256])
-        dsend[half] = product.astype(BF16).reshape(NX, 32, 256)
-        for n, k in enumerate(reversed(x_order)):
-            peer = lax.rem(x + k, NX)
-            copy = remote(
-                dsend.at[half, peer],
-                drecv.at[half, x],
-                ds_sem.at[half, n],
-                dr_sem.at[half, x],
-                at(0, k),
-            )
-            copy.start()
-            sends.append(copy)
-    drecv[:, x] = dsend[:, x]
+    dsend[...] = dot(ot[...], bd[...]).astype(BF16).reshape(NX, 32, 512)
+    for n, k in enumerate(reversed(x_order)):
+        peer = lax.rem(x + k, NX)
+        copy = remote(dsend.at[peer], drecv.at[x], ds_sem.at[n], dr_sem.at[x], at(0, k))
+        copy.start()
+        sends.append(copy)
+    drecv[x] = dsend[x]
     for k in [0] + x_order:
         peer = lax.rem(x + k, NX)
-        for half in range(2):
-            if k:
-                block = drecv.at[half, peer]
-                remote(
-                    block, block, ds_sem.at[half, 0], dr_sem.at[half, peer], me
-                ).wait_recv()
-            block = drecv[half, peer].astype(F32)
-            for i in range(2):
-                for j in range(4):
-                    f32s[pl.ds((half * 2 + i) * 128 + peer * 4 + j, 8, stride=16), :] = block[
-                        j * 8 : (j + 1) * 8, i * 128 : (i + 1) * 128
-                    ]
+        if k:
+            block = drecv.at[peer]
+            remote(block, block, ds_sem.at[0], dr_sem.at[peer], me).wait_recv()
+        block = drecv[peer].astype(F32)
+        for i in range(4):
+            for j in range(4):
+                f32s[pl.ds(i * 128 + peer * 4 + j, 8, stride=16), :] = block[
+                    j * 8 : (j + 1) * 8, i * 128 : (i + 1) * 128
+                ]
     pair_out[...] = (f32s[...] + two_v[...].reshape(512, 128).astype(F32)).astype(BF16).reshape(4, 128, 128)
     for copy in sends:
         copy.wait_send()
+
+
+def write_out(align, pair, align_out, pair_out, sem):
+    copies = [
+        pltpu.make_async_copy(align, align_out, sem.at[0]),
+        pltpu.make_async_copy(pair, pair_out, sem.at[1]),
+    ]
+    for copy in copies:
+        copy.start()
+    for copy in copies:
+        copy.wait()
 
 
 def per_device(hom, two, offset_map, win, wout, cwin, cwout, factors, tpe):
@@ -439,8 +439,8 @@
         vm((128, 4096), BF16),
         vm((1024, 128), F32),
         vm((4096, 512), BF16),
-        vm((2, NX, 32, 256), BF16),
-        vm((2, NX, 32, 256), BF16),
+        vm((NX, 32, 512), BF16),
+        vm((NX, 32, 512), BF16),
         vm((512, 128), F32),
         dma((9,)),
         dma((31,)),
@@ -451,8 +451,8 @@
         dma((2, NX)),
         dma((2, 7)),
         dma((2, NY)),
-        dma((2, 3)),
-        dma((2, NX)),
+        dma((3,)),
+        dma((NX,)),
     ]
     hbm = pl.BlockSpec(memory_space=pl.ANY)
     align, pair = pl.pallas_call(
@@ -466,7 +466,17 @@
         scratch_shapes=scratch,
         compiler_params=pltpu.CompilerParams(collective_id=0, has_side_effects=True, vmem_limit_bytes=40 * 2**20),
     )(*operands)
-    return align, pair
+    return pl.pallas_call(
+        write_out,
+        out_shape=(
+            jax.ShapeDtypeStruct((128, 4, 256), BF16),
+            jax.ShapeDtypeStruct((4, 128, 128), BF16),
+        ),
+        in_specs=[pl.BlockSpec(memory_space=pltpu.VMEM)] * 2,
+        out_specs=(hbm, hbm),
+        scratch_shapes=[dma((2,))],
+        compiler_params=pltpu.CompilerParams(vmem_limit_bytes=40 * 2**20),
+    )(align, pair)
 
 
 def solution(mesh):

time: 44.2 us -> 43.2 us (0.977)
  local copies, waits for them, and re-layouts: 1.36 us -> 0 us
  Pallas kernels: 42 us -> 42.5 us
    unnamed x2 -> x0, local copies, waits for them, and re-layouts: 1.36 us -> none
    pallas_call x0 -> x1, Pallas kernels: none -> 0.76 us  [per_device(): pl.pallas_call(write_out, out_shape=(jax.ShapeDtypeStruct((128, 4, 256),...]
where the time goes in v5:
time: 43.2 us; the launch traced here: 43.1 us
  Pallas kernels  42.5 us (98%)
  between operations  0.64 us (1%)
    pallas_call x1, Pallas kernels, per_device(): pl.pallas_call(kernel, out_shape=(jax.ShapeDtypeStruct((128, 4, 256), BF1...  41.7 us

profile of v5, /device:TPU:448, one launch (start us, length us, event | category | flops | bytes accessed | tf_op | source)
XLA Modules:
  0.0 43.1 jit_solution(3664256408113308512)
XLA Ops:
  0.6 41.7 %shard_map.104 = (bf16[128,4,256]{2,1,0:T(4,128)(2,1)S(1)}, bf16[4,128,128]{2,1,0:T(8,128)(2,1)S(1)}) custom-call(bf16[4,128,256]{2,1,0:T(8,128)(2,1)} %hom.1, bf16[4,128,128]{2,1,0:T(8,128)(2,1)} %two.1, bf16[8,128]{1,0:T(8,128)(2,1)} %bitcast.3, bf16[256,1024]{1,0:T(8,128)(2,1)} %win.1, bf16[256,256]{1,0:T(8,128)(2,1)} %wout.1, bf16[256,1024]{1,0:T(8,128)(2,1)} %cwin.1, ...), custom_call_target="tpu_custom_call" | custom-call | tf_op jit(solution)/shard_map/pallas_call | solution.py:458
  42.3 0.8 %shard_map.105 = (bf16[128,4,256]{2,1,0:T(4,128)(2,1)}, bf16[4,128,128]{2,1,0:T(8,128)(2,1)}) custom-call(bf16[128,4,256]{2,1,0:T(4,128)(2,1)S(1)} %get-tuple-element.4.align, bf16[4,128,128]{2,1,0:T(8,128)(2,1)S(1)} %get-tuple-element.5.pair), custom_call_target="tpu_custom_call" | custom-call | tf_op jit(solution)/shard_map/pallas_call | solution.py:469

commit v6 on v5

--- a/solution.py
+++ b/solution.py
@@ -89,6 +89,7 @@
     k_s,
     v_s,
     g_s,
+    sc,
     xp,
     b32,
     bias_recv,
@@ -216,6 +217,17 @@
     for group in range(NX):
         xp[group] = mixed(x32, group)
 
+    scale = LOG2E / math.sqrt(32)
+    for s in range(4):
+        rows = slice(s * 32, (s + 1) * 32)
+        for g in range(2):
+            lanes = slice(g * 128, (g + 1) * 128)
+            query = jnp.concatenate(
+                [q_s[c, rows, lanes] * mask for c in range(NX) for mask in masks], axis=0
+            )
+            scores = dot_nt(query, k_s[s * 128 : (s + 1) * 128, lanes]) * scale
+            sc[:, g, s] = scores.reshape(NX, 128, 128)
+
     ready["tpe"].wait()
     w32[...] = tpe_v[...].astype(F32)
     bd[...] = jnp.zeros_like(bd)
@@ -231,7 +243,6 @@
             send_bias(block, at(0, m))
 
     ready["wout"].wait()
-    scale = LOG2E / math.sqrt(32)
     ones = jnp.ones((128, 128), BF16)
     for n, m in enumerate([0, 1, 2, 3]):
         column = lax.rem(x + m, NX)
@@ -252,9 +263,7 @@
             part = []
             for s in range(4):
                 rows = slice(s * 32, (s + 1) * 32)
-                query = q_s[column, rows, lanes]
-                query = jnp.concatenate([query * mask for mask in masks], axis=0)
-                scores = dot_nt(query, k_s[s * 128 : (s + 1) * 128, lanes]) * scale + bias[g]
+                scores = sc[column, g, s] + bias[g]
                 highest = jnp.max(scores, axis=-1, keepdims=True)
                 weights = jnp.exp2(scores - highest).astype(BF16)
                 value = jnp.concatenate([v_s[s * 128 : (s + 1) * 128, lanes], ones], axis=1)
@@ -311,6 +320,7 @@
     remote(everything, everything, ms_sem, mr_sem.at[0], me).wait_send()
 
     sends = []
+    done = []
     for half in range(2):
         pair = (half * 2, half * 2 + 1)
         rows = slice(half * 256, (half + 1) * 256)
@@ -346,11 +356,13 @@
             )
         for copy in sends[start:]:
             copy.start()
-        for n, r in enumerate(pair):
-            for c in range(NX):
-                for d in range(NY):
-                    begin = n * 128 + c * 32 + d * 4
-                    put(y32, (d * NX + c) * 16 + r, 4, wide[begin : begin + 4], stride=4)
+        done.append(wide)
+    for r in range(4):
+        wide = done[r // 2]
+        for c in range(NX):
+            for d in range(NY):
+                begin = (r % 2) * 128 + c * 32 + d * 4
+                put(y32, (d * NX + c) * 16 + r, 4, wide[begin : begin + 4], stride=4)
 
     align_out[...] = jnp.concatenate([y32[0], y32[1]], axis=1).reshape(128, 4, 256).astype(BF16)
 
@@ -426,6 +438,7 @@
         vm((512, 256), BF16),
         vm((512, 256), BF16),
         vm((NX, 128, 256), F32),
+        vm((NX, 2, 4, 128, 128), F32),
         vm((NX, 128, 256), F32),
         vm((NX, 256, 128), F32),
         vm((ND, 32, 128), BF16),

time: 43.2 us -> 42.1 us (0.975); the launches traced: 43.1 us -> 41.6 us
  Pallas kernels: 42.5 us -> 40.9 us
    pallas_call x1, Pallas kernels: 41.7 us -> 40.2 us  [per_device(): pl.pallas_call(kernel, out_shape=(jax.ShapeDtypeStruct((128, 4, 256), BF1...]
where the time goes in v6:
time: 42.1 us; the launch traced here: 41.6 us
  Pallas kernels  40.9 us (97%)
  between operations  0.64 us (2%)
    pallas_call x1, Pallas kernels, per_device(): pl.pallas_call(kernel, out_shape=(jax.ShapeDtypeStruct((128, 4, 256), BF1...  40.2 us

profile of v6, /device:TPU:448, one launch (start us, length us, event | category | flops | bytes accessed | tf_op | source)
XLA Modules:
  0.0 41.6 jit_solution(11839268269560808239)
XLA Ops:
  0.6 40.2 %shard_map.104 = (bf16[128,4,256]{2,1,0:T(4,128)(2,1)S(1)}, bf16[4,128,128]{2,1,0:T(8,128)(2,1)S(1)}) custom-call(bf16[4,128,256]{2,1,0:T(8,128)(2,1)} %hom.1, bf16[4,128,128]{2,1,0:T(8,128)(2,1)} %two.1, bf16[8,128]{1,0:T(8,128)(2,1)} %bitcast.3, bf16[256,1024]{1,0:T(8,128)(2,1)} %win.1, bf16[256,256]{1,0:T(8,128)(2,1)} %wout.1, bf16[256,1024]{1,0:T(8,128)(2,1)} %cwin.1, ...), custom_call_target="tpu_custom_call" | custom-call | tf_op jit(solution)/shard_map/pallas_call | solution.py:471
  40.8 0.8 %shard_map.105 = (bf16[128,4,256]{2,1,0:T(4,128)(2,1)}, bf16[4,128,128]{2,1,0:T(8,128)(2,1)}) custom-call(bf16[128,4,256]{2,1,0:T(4,128)(2,1)S(1)} %get-tuple-element.4.align, bf16[4,128,128]{2,1,0:T(8,128)(2,1)S(1)} %get-tuple-element.5.pair), custom_call_target="tpu_custom_call" | custom-call | tf_op jit(solution)/shard_map/pallas_call | solution.py:482

commit v7 on v6

--- a/solution.py
+++ b/solution.py
@@ -50,14 +50,15 @@
 
 def attend(q, k, v, gate, masks):
     scale = LOG2E / math.sqrt(32)
-    weights = []
-    values = []
-    for h in range(4):
-        scores = dot_nt(q * masks[h], k) * scale
-        highest = jnp.max(scores, axis=-1, keepdims=True)
-        weights.append(jnp.exp2(scores - highest).astype(BF16))
-        ones = jnp.broadcast_to(masks[h], v.shape)
-        values.append(jnp.concatenate([v * masks[h], ones], axis=1))
+    rows = q.shape[0]
+    query = jnp.concatenate([q * mask for mask in masks], axis=0)
+    scores = dot_nt(query, k) * scale
+    highest = jnp.max(scores, axis=-1, keepdims=True)
+    stacked = jnp.exp2(scores - highest).astype(BF16)
+    weights = [stacked[h * rows : (h + 1) * rows] for h in range(4)]
+    values = [
+        jnp.concatenate([v * mask, jnp.broadcast_to(mask, v.shape)], axis=1) for mask in masks
+    ]
     both = dot(jnp.concatenate(weights, axis=1), jnp.concatenate(values, axis=0))
     return (jax.nn.sigmoid(gate) * (both[:, :128] / both[:, 128:])).astype(BF16)
 

time: 42.1 us -> 40.9 us (0.971)
  Pallas kernels: 40.9 us -> 39.8 us
    pallas_call x1, Pallas kernels: 40.2 us -> 39 us  [per_device(): pl.pallas_call(kernel, out_shape=(jax.ShapeDtypeStruct((128, 4, 256), BF1...]
where the time goes in v7:
time: 40.9 us; the launch traced here: 40.4 us
  Pallas kernels  39.8 us (97%)
  between operations  0.64 us (2%)
    pallas_call x1, Pallas kernels, per_device(): pl.pallas_call(kernel, out_shape=(jax.ShapeDtypeStruct((128, 4, 256), BF1...  39 us

profile of v7, /device:TPU:448, one launch (start us, length us, event | category | flops | bytes accessed | tf_op | source)
XLA Modules:
  0.0 40.4 jit_solution(17535763992879129723)
XLA Ops:
  0.6 39.0 %shard_map.104 = (bf16[128,4,256]{2,1,0:T(4,128)(2,1)S(1)}, bf16[4,128,128]{2,1,0:T(8,128)(2,1)S(1)}) custom-call(bf16[4,128,256]{2,1,0:T(8,128)(2,1)} %hom.1, bf16[4,128,128]{2,1,0:T(8,128)(2,1)} %two.1, bf16[8,128]{1,0:T(8,128)(2,1)} %bitcast.3, bf16[256,1024]{1,0:T(8,128)(2,1)} %win.1, bf16[256,256]{1,0:T(8,128)(2,1)} %wout.1, bf16[256,1024]{1,0:T(8,128)(2,1)} %cwin.1, ...), custom_call_target="tpu_custom_call" | custom-call | tf_op jit(solution)/shard_map/pallas_call | solution.py:472
  39.7 0.8 %shard_map.105 = (bf16[128,4,256]{2,1,0:T(4,128)(2,1)}, bf16[4,128,128]{2,1,0:T(8,128)(2,1)}) custom-call(bf16[128,4,256]{2,1,0:T(4,128)(2,1)S(1)} %get-tuple-element.4.align, bf16[4,128,128]{2,1,0:T(8,128)(2,1)S(1)} %get-tuple-element.5.pair), custom_call_target="tpu_custom_call" | custom-call | tf_op jit(solution)/shard_map/pallas_call | solution.py:483
